TPU v7x, 32 devices: a whole 2x2x4 slice. The times are simulated.
32 devices in a mesh: grp: 4 (over z), seq: 8 (over y, x, core).
Axes of the slice: x: 2, y: 2, z: 4, core: 2. Of those that a mesh axis runs over, the one named last changes fastest.
Arguments:
- fine_rows: bfloat16 [4, 1024, 2048], P('grp', 'seq'), may hold values from -6 to 6
- segment_ids: int32 [4, 1024], P('grp', 'seq'), may hold values from 0 to 7, as said below
- pool_gain: float32 [2048], replicated, may hold values from 0.1 to 1.9
- w_in: bfloat16 [2048, 8192], P('grp', 'seq'), may hold values from -0.125 to 0.125
- w_gate: bfloat16 [8192, 16384], P('grp', 'seq'), may hold values from -0.0625 to 0.0625
- w_up: bfloat16 [8192, 16384], P('grp', 'seq'), may hold values from -0.0625 to 0.0625
- w_down: bfloat16 [16384, 8192], P('seq', 'grp'), may hold values from -0.046875 to 0.046875
- out_grad: bfloat16 [4, 64, 8192], P('grp'), may hold values from -6 to 6
Outputs:
- coarse_out: bfloat16 [4, 64, 8192], P('grp', None, 'seq')
- fine_grad: bfloat16 [4, 1024, 2048], P('grp', 'seq')
Inputs may be any that keep to these rules, and one draw needn't show every extreme that they name: `segment_ids`: within each shard of 128 consecutive bytes the numbers count the shard's segments from 0 upward, never falling, every segment one byte or more; a shard holds 4 to 8 segments, some shard of every document exactly 8, and every document 48 segments in all.
All inputs are finite; a program needn't handle non-finite values.
Results may differ from a plain program's by a relative error of at most 0.02.
Values may be sent and summed in bfloat16 or wider, within the bound.
A program may use at most 192 MiB of HBM per device.

v0:
```python
import jax
import jax.numpy as jnp
from jax import lax
from jax.sharding import PartitionSpec as P

SEG_CAP = 8
norm_eps = 1e-06
bf16 = jnp.bfloat16
f32 = jnp.float32


def silu_parts(gate_value):
    sigma = jax.nn.sigmoid(gate_value)
    return (gate_value * sigma, sigma * (1.0 + gate_value * (1.0 - sigma)))


def matmul(a, b):
    return jnp.dot(a, b, preferred_element_type=f32)


def matmul_t(a, b):
    return lax.dot_general(a, b, (((1,), (1,)), ((), ())), preferred_element_type=f32)


def swap_pairs(grps, seqs):
    halves = seqs // grps
    return [
        (g * seqs + p * halves + h, p * seqs + g * halves + h)
        for g in range(grps)
        for p in range(grps)
        for h in range(halves)
    ]


def grp_total(partial_value):
    return lax.psum_scatter(
        partial_value.astype(bf16), "grp", scatter_dimension=0, tiled=True
    ).astype(f32)


def make_shards(grps, seqs):
    halves = seqs // grps
    pairs = swap_pairs(grps, seqs)

    def swap(value):
        return lax.ppermute(value, ("grp", "seq"), pairs)

    def shards(fine_rows, segment_ids, pool_gain, w_in, w_gate, w_up, w_down, out_grad):
        rows_here = fine_rows[0]
        index_here = segment_ids[0]
        feat, width = w_in.shape
        slots = jnp.arange(SEG_CAP, dtype=jnp.int32)
        member = index_here[None, :] == slots[:, None]
        segment_sums = matmul(member.astype(bf16), rows_here)
        inv_rms = lax.rsqrt(jnp.mean(segment_sums * segment_sums, axis=1, keepdims=True) + norm_eps)
        pooled = (segment_sums * inv_rms * pool_gain).astype(bf16)
        live_count = jnp.max(index_here) + 1
        packed = jnp.concatenate(
            [pooled, jnp.full((1, pooled.shape[1]), live_count.astype(bf16))], axis=0
        )
        gathered = lax.all_gather(packed, "seq", axis=0)
        shard_counts = gathered[:, SEG_CAP, 0].astype(jnp.int32)
        gathered = gathered[:, :SEG_CAP].reshape(seqs * SEG_CAP, -1)
        offsets = jnp.cumsum(shard_counts) - shard_counts
        slot_count = seqs * SEG_CAP
        within = jnp.tile(slots, seqs)
        target = jnp.repeat(offsets, SEG_CAP) + within
        is_live = within < jnp.repeat(shard_counts, SEG_CAP)
        rows = slot_count * 3 // 4
        select = (target[None, :] == jnp.arange(rows, dtype=jnp.int32)[:, None]) & is_live[None, :]
        selector = select.astype(bf16)
        work_in = matmul(selector, gathered).astype(bf16)
        work_in = lax.all_to_all(
            work_in.reshape(rows, grps, feat), "grp", split_axis=1, concat_axis=0
        ).reshape(grps * rows, feat)
        x_cols = grp_total(matmul(work_in, w_in)).astype(bf16)
        seq_at = lax.axis_index("seq")
        block = w_gate.shape[0]
        piece = block // seqs
        grad_here = out_grad[0].reshape(slot_count, grps, seqs, piece)
        grad_part = lax.dynamic_index_in_dim(grad_here, seq_at, 2, keepdims=False)
        grad_part = matmul(selector, grad_part.reshape(slot_count, grps * piece)).astype(bf16)
        grad_part = lax.all_to_all(
            grad_part.reshape(rows, grps, piece), "grp", split_axis=1, concat_axis=0
        ).reshape(grps * rows, piece)
        work_grad = lax.all_gather(grad_part, "seq", axis=1, tiled=True)
        grad_hidden = grp_total(matmul_t(work_grad, w_down))

        def spread(cols):
            every = lax.all_gather(swap(cols), "seq", axis=0)
            every = every.reshape(grps, halves, rows, width)
            return every.transpose(0, 2, 1, 3).reshape(grps * rows, halves * width)

        def column_total(part):
            part = part.astype(bf16).reshape(grps, rows, halves, width)
            part = part.transpose(0, 2, 1, 3).reshape(seqs * rows, width)
            return swap(lax.psum_scatter(part, "seq", scatter_dimension=0, tiled=True)).astype(f32)

        coarse_x = spread(x_cols)
        gate_value = grp_total(matmul(coarse_x, w_gate))
        up_value = grp_total(matmul(coarse_x, w_up))
        activated, derivative = silu_parts(gate_value)
        hidden = (activated * up_value).astype(bf16)
        grad_gate = (grad_hidden * up_value * derivative).astype(bf16)
        grad_up = (grad_hidden * activated).astype(bf16)
        grad_gate = lax.all_gather(grad_gate, "grp", axis=0, tiled=True)
        grad_up = lax.all_gather(grad_up, "grp", axis=0, tiled=True)
        hidden = lax.all_gather(hidden, "grp", axis=0, tiled=True)
        back_cols = column_total(matmul_t(grad_gate, w_gate) + matmul_t(grad_up, w_up))
        down_cols = column_total(matmul(hidden, w_down))
        out_cols = (x_cols.astype(f32) + down_cols).astype(bf16)
        out_cols = matmul(selector.T, out_cols).astype(bf16)
        grad_cols = lax.dynamic_slice_in_dim(out_grad[0], seq_at * width, width, 1)
        grad_cols = matmul(selector, grad_cols)
        grad_x = (back_cols + grad_cols).astype(bf16)
        grad_x = lax.all_gather(grad_x, "grp", axis=0, tiled=True)
        term = matmul_t(grad_x, w_in).astype(bf16)
        term = lax.all_to_all(
            term.reshape(grps, rows, feat), "grp", split_axis=0, concat_axis=1
        ).reshape(rows, grps * feat)
        term = matmul(selector.T, term).astype(bf16)
        grad_pooled = lax.psum_scatter(term, "seq", scatter_dimension=0, tiled=True).astype(f32)
        weighted = grad_pooled * pool_gain
        inner = jnp.mean(weighted * segment_sums, axis=1, keepdims=True)
        grad_sums = inv_rms * weighted - segment_sums * (inv_rms * inv_rms * inv_rms) * inner
        fine_grad = matmul(member.astype(bf16).T, grad_sums.astype(bf16)).astype(bf16)
        return (out_cols[None], fine_grad[None])

    return shards


def solution(mesh):
    return jax.shard_map(
        make_shards(mesh.shape["grp"], mesh.shape["seq"]),
        mesh=mesh,
        in_specs=(
            P("grp", "seq", None),
            P("grp", "seq"),
            P(),
            P("grp", "seq"),
            P("grp", "seq"),
            P("grp", "seq"),
            P("seq", "grp"),
            P("grp", None, None),
        ),
        out_specs=(P("grp", None, "seq"), P("grp", "seq", None)),
        check_vma=False,
    )
```

profile of v0, /device:TPU:0, one launch (start us, length us, event | category | flops | bytes accessed | tf_op | source)
XLA Modules:
  0.0 326.0 jit_solution(11023302746642176019)
XLA Ops:
  7.2 1.4 multiply_reduce_fusion.1
  8.6 1.3 reduce_max.9
  10.6 0.8 multiply_convert_fusion
  11.4 11.3 %all-gather.2 = bf16[8,9,2048]{2,1,0:T(8,128)(2,1)S(1)} all-gather(bf16[1,9,2048]{2,1,0:T(8,128)(2,1)S(1)} %pad_bitcast_fusion), channel_id=2, replica_groups=mesh['grp'=4,'seq'=8] {'seq'}, dimensions={0}, use_global_device_ids=true | all-gather | bytes 331776 | tf_op jit(solution)/shard_map/all_gather | solution.py:61
  22.7 0.2 fusion.39
  23.4 0.2 convolution_convert_fusion.6
  23.8 0.7 copy.18
  24.5 4.9 %all-to-all-start = ((bf16[1,48,4,512]{3,1,0,2:T(8,128)(2,1)}), bf16[1,48,4,512]{3,1,0,2:T(8,128)(2,1)S(1)}, u32[]{:S(2)}, u32[]{:S(2)}) async-start(bf16[1,48,4,512]{3,1,0,2:T(8,128)(2,1)} %copy.18), calls=%async_computation | async-start | bytes 393216 | tf_op jit(solution)/shard_map/all_to_all | solution.py:73
  29.4 1.5 copy.28
  30.9 0.8 dynamic-slice_reduce_fusion
  31.9 0.7 copy.22
  32.6 4.8 %all-to-all-done = bf16[1,48,4,512]{3,1,0,2:T(8,128)(2,1)S(1)} async-done(((bf16[1,48,4,512]{3,1,0,2:T(8,128)(2,1)}), bf16[1,48,4,512]{3,1,0,2:T(8,128)(2,1)S(1)}, u32[]{:S(2)}, u32[]{:S(2)}) %all-to-all-start) | async-done | bytes 196640 | tf_op jit(solution)/shard_map/all_to_all | solution.py:73
  37.4 3.3 %all-to-all-start.1 = ((bf16[1,48,4,256]{3,1,0,2:T(8,128)(2,1)}), bf16[1,48,4,256]{3,1,0,2:T(8,128)(2,1)S(1)}, u32[]{:S(2)}, u32[]{:S(2)}) async-start(bf16[1,48,4,256]{3,1,0,2:T(8,128)(2,1)} %copy.22), calls=%async_computation.5 | async-start | bytes 196608 | tf_op jit(solution)/shard_map/all_to_all | solution.py:83
  40.7 1.1 convolution_convert_fusion.7
  41.9 4.5 %all-to-all-done.1 = bf16[1,48,4,256]{3,1,0,2:T(8,128)(2,1)S(1)} async-done(((bf16[1,48,4,256]{3,1,0,2:T(8,128)(2,1)}), bf16[1,48,4,256]{3,1,0,2:T(8,128)(2,1)S(1)}, u32[]{:S(2)}, u32[]{:S(2)}) %all-to-all-start.1) | async-done | bytes 98336 | tf_op jit(solution)/shard_map/all_to_all | solution.py:83
  46.5 11.9 %all_gather.32 = bf16[192,2048]{1,0:T(8,128)(2,1)S(1)} all-gather(bf16[192,256]{1,0:T(8,128)(2,1)S(1)} %bitcast.93), channel_id=1, replica_groups=mesh['grp'=4,'seq'=8] {'seq'}, dimensions={1}, use_global_device_ids=true | all-gather | bytes 884736 | tf_op jit(solution)/shard_map/all_gather | solution.py:86
  58.4 7.2 %convolution_convert_fusion = bf16[192,2048]{1,0:T(8,128)(2,1)} fusion(bf16[192,2048]{1,0:T(8,128)(2,1)S(1)} %all_gather.32, bf16[2048,2048]{1,0:T(8,128)(2,1)} %param.14), kind=kOutput, calls=%fused_computation.1 | convolution fusion | flops 1611005952 | bytes 9961472 | tf_op jit(solution)/shard_map/dot_general | solution.py:22
  65.7 1.6 collective-permute-start
  67.3 27.1 %all-gather.1 = bf16[384,1024]{1,0:T(8,128)(2,1)S(1)} all-gather(bf16[48,1024]{1,0:T(8,128)(2,1)S(1)} %collective-permute-done), channel_id=3, replica_groups=mesh['grp'=4,'seq'=8] {'seq'}, dimensions={0}, use_global_device_ids=true | all-gather | bytes 884736 | tf_op jit(solution)/shard_map/all_gather | solution.py:90
  94.4 0.8 copy.19
  95.5 6.1 %convolution_convert_fusion.3 = bf16[192,2048]{1,0:T(8,128)(2,1)} fusion(bf16[192,2048]{1,0:T(8,128)(2,1)S(1)} %bitcast.87, bf16[2048,2048]{1,0:T(8,128)(2,1)} %param.12), kind=kOutput, calls=%fused_computation.4 | convolution fusion | flops 1611005952 | bytes 9961472 | tf_op jit(solution)/shard_map/dot_general | solution.py:18
  101.6 6.1 %convolution_convert_fusion.2 = bf16[192,2048]{1,0:T(8,128)(2,1)} fusion(bf16[192,2048]{1,0:T(8,128)(2,1)S(1)} %bitcast.88, bf16[2048,2048]{1,0:T(8,128)(2,1)} %param.13), kind=kOutput, calls=%fused_computation.3 | convolution fusion | flops 1611005952 | bytes 9961472 | tf_op jit(solution)/shard_map/dot_general | solution.py:18
  107.8 14.5 %reduce-scatter.10.cloned.1.call-done = bf16[48,2048]{1,0:T(8,128)(2,1)} async-done(((bf16[192,2048]{1,0:T(8,128)(2,1)}), bf16[48,2048]{1,0:T(8,128)(2,1)}) %reduce-scatter.10.cloned.1.call-update) | async-done | bytes 196624 | tf_op jit(solution)/shard_map/reduce_scatter | solution.py:36
  122.3 24.9 %reduce-scatter.12.cloned.1.call-done = bf16[48,2048]{1,0:T(8,128)(2,1)} async-done(((bf16[192,2048]{1,0:T(8,128)(2,1)}), bf16[48,2048]{1,0:T(8,128)(2,1)}) %reduce-scatter.12.cloned.1.call-update) | async-done | bytes 196624 | tf_op jit(solution)/shard_map/reduce_scatter | solution.py:36
  147.1 1.4 fusion.8
  148.5 18.2 %all_gather.33 = bf16[192,2048]{1,0:T(8,128)(2,1)S(1)} all-gather(bf16[48,2048]{1,0:T(8,128)(2,1)S(1)} %get-tuple-element.3), channel_id=1, replica_groups=mesh['grp'=4,'seq'=8] {'grp'}, dimensions={0}, use_global_device_ids=true | all-gather | bytes 983040 | tf_op jit(solution)/shard_map/all_gather | solution.py:106
  166.7 6.3 %fusion.43 = f32[192,2048]{1,0:T(8,128)S(1)} fusion(bf16[192,2048]{1,0:T(8,128)(2,1)S(1)} %all_gather.33, bf16[2048,2048]{1,0:T(8,128)(2,1)} %param.12), kind=kOutput, calls=%fused_computation.73 | convolution fusion | flops 1610612736 | bytes 10747904 | tf_op jit(solution)/shard_map/dot_general | solution.py:22
  173.0 17.4 %all_gather.34 = bf16[192,2048]{1,0:T(8,128)(2,1)S(1)} all-gather(bf16[48,2048]{1,0:T(8,128)(2,1)S(1)} %get-tuple-element.2), channel_id=1, replica_groups=mesh['grp'=4,'seq'=8] {'grp'}, dimensions={0}, use_global_device_ids=true | all-gather | bytes 983040 | tf_op jit(solution)/shard_map/all_gather | solution.py:107
  190.4 6.3 %fusion = bf16[192,2048]{1,0:T(8,128)(2,1)S(1)} fusion(f32[192,2048]{1,0:T(8,128)S(1)} %fusion.43, bf16[192,2048]{1,0:T(8,128)(2,1)S(1)} %all_gather.34, bf16[2048,2048]{1,0:T(8,128)(2,1)} %param.13), kind=kOutput, calls=%fused_computation.5 | convolution fusion | flops 1611399168 | bytes 11534336 | tf_op jit(solution)/shard_map/dot_general | solution.py:22
  196.7 0.6 reshape.115
  197.2 1.1 copy.23
  198.4 16.8 %all_gather.31 = bf16[192,2048]{1,0:T(8,128)(2,1)S(1)} all-gather(bf16[48,2048]{1,0:T(8,128)(2,1)S(1)} %get-tuple-element.4), channel_id=1, replica_groups=mesh['grp'=4,'seq'=8] {'grp'}, dimensions={0}, use_global_device_ids=true | all-gather | bytes 983040 | tf_op jit(solution)/shard_map/all_gather | solution.py:108
  215.2 18.1 %reduce-scatter.18.cloned.1.call-done = bf16[48,1024]{1,0:T(8,128)(2,1)} async-done(((bf16[384,1024]{1,0:T(8,128)(2,1)}), bf16[48,1024]{1,0:T(8,128)(2,1)}) %reduce-scatter.18.cloned.1.call-update) | async-done | bytes 98320 | tf_op jit(solution)/shard_map/reduce_scatter | solution.py:97
  233.4 1.5 collective-permute-start.2
  234.9 5.2 %convolution_convert_fusion.1 = bf16[192,2048]{1,0:T(8,128)(2,1)S(1)} fusion(bf16[192,2048]{1,0:T(8,128)(2,1)S(1)} %all_gather.31, bf16[2048,2048]{1,0:T(8,128)(2,1)} %param.14), kind=kOutput, calls=%fused_computation.2 | convolution fusion | flops 1611005952 | bytes 9961472 | tf_op jit(solution)/shard_map/dot_general | solution.py:18
  240.1 0.6 reshape.112
  240.7 1.1 copy.20
  241.9 1.1 add_convert_fusion
  243.0 16.2 %all_gather.35 = bf16[192,1024]{1,0:T(8,128)(2,1)S(1)} all-gather(bf16[48,1024]{1,0:T(8,128)(2,1)S(1)} %add_convert_fusion), channel_id=1, replica_groups=mesh['grp'=4,'seq'=8] {'grp'}, dimensions={0}, use_global_device_ids=true | all-gather | bytes 491520 | tf_op jit(solution)/shard_map/all_gather | solution.py:116
  259.1 0.5 convolution_convert_fusion.8
  259.6 11.9 %all_to_all.45 = bf16[4,48,1,512]{3,1,2,0:T(8,128)(2,1)S(1)} all-to-all(bf16[4,48,1,512]{3,1,2,0:T(8,128)(2,1)S(1)} %bitcast.85), channel_id=1, replica_groups=mesh['grp'=4,'seq'=8] {'grp'}, dimensions={0} | all-to-all | bytes 393216 | tf_op jit(solution)/shard_map/all_to_all | solution.py:118
  271.7 1.0 convolution_convert_fusion.5
  272.7 6.1 %reduce-scatter.14.cloned.1.call-done = bf16[48,1024]{1,0:T(8,128)(2,1)} async-done(((bf16[384,1024]{1,0:T(8,128)(2,1)}), bf16[48,1024]{1,0:T(8,128)(2,1)}) %reduce-scatter.14.cloned.1.call-update) | async-done | bytes 98320 | tf_op jit(solution)/shard_map/reduce_scatter | solution.py:97
  278.8 1.5 collective-permute-start.1
  280.3 0.9 fusion.2
  281.2 35.1 %reduce-scatter.20.cloned.1.call-done = bf16[8,2048]{1,0:T(8,128)(2,1)} async-done(((bf16[64,2048]{1,0:T(8,128)(2,1)}), bf16[8,2048]{1,0:T(8,128)(2,1)}) %reduce-scatter.20.cloned.1.call-update) | async-done | bytes 32784 | tf_op jit(solution)/shard_map/reduce_scatter | solution.py:122
  316.3 0.9 multiply_reduce_fusion
  317.2 1.9 fusion.1
  (43 shorter events, 1.7 us)
Async XLA Ops:
  7.2 33.6 %copy-start = (bf16[512,1024]{1,0:T(8,128)(2,1)S(1)}, bf16[512,1024]{1,0:T(8,128)(2,1)}, u32[]{:S(2)}) copy-start(bf16[512,1024]{1,0:T(8,128)(2,1)} %param.11) | copy-start | bytes 3145732
  24.5 12.9 %all-to-all-start = ((bf16[1,48,4,512]{3,1,0,2:T(8,128)(2,1)}), bf16[1,48,4,512]{3,1,0,2:T(8,128)(2,1)S(1)}, u32[]{:S(2)}, u32[]{:S(2)}) async-start(bf16[1,48,4,512]{3,1,0,2:T(8,128)(2,1)} %copy.18), calls=%async_computation | async-start | bytes 393216 | tf_op jit(solution)/shard_map/all_to_all | solution.py:73
  37.4 9.1 %all-to-all-start.1 = ((bf16[1,48,4,256]{3,1,0,2:T(8,128)(2,1)}), bf16[1,48,4,256]{3,1,0,2:T(8,128)(2,1)S(1)}, u32[]{:S(2)}, u32[]{:S(2)}) async-start(bf16[1,48,4,256]{3,1,0,2:T(8,128)(2,1)} %copy.22), calls=%async_computation.5 | async-start | bytes 196608 | tf_op jit(solution)/shard_map/all_to_all | solution.py:83
  40.7 25.1 %reduce-scatter.8.cloned.1.call-start = ((), (), s32[]{:S(2)}) async-start(), calls=%async_computation.10 | async-start | bytes 491520 | tf_op jit(solution)/shard_map/reduce_scatter | solution.py:36
  41.9 65.9 %reduce-scatter.16.cloned.1.call-start = ((), (), s32[]{:S(2)}) async-start(), calls=%async_computation.14 | async-start | bytes 983040 | tf_op jit(solution)/shard_map/reduce_scatter | solution.py:36
  65.7 56.6 %reduce-scatter.10.cloned.1.call-start = ((), (), s32[]{:S(2)}) async-start(), calls=%async_computation.11 | async-start | bytes 983040 | tf_op jit(solution)/shard_map/reduce_scatter | solution.py:36
  65.7 1.6 collective-permute-start
  101.6 45.6 %reduce-scatter.12.cloned.1.call-start = ((), (), s32[]{:S(2)}) async-start(), calls=%async_computation.12 | async-start | bytes 983040 | tf_op jit(solution)/shard_map/reduce_scatter | solution.py:36
  107.7 125.6 %reduce-scatter.18.cloned.1.call-start = ((), (), s32[]{:S(2)}) async-start(), calls=%async_computation.15 | async-start | bytes 884736 | tf_op jit(solution)/shard_map/reduce_scatter | solution.py:97
  198.4 80.4 %reduce-scatter.14.cloned.1.call-start = ((), (), s32[]{:S(2)}) async-start(), calls=%async_computation.13 | async-start | bytes 884736 | tf_op jit(solution)/shard_map/reduce_scatter | solution.py:97
  215.2 65.1 %copy-start.1 = (bf16[48,1024]{1,0:T(8,128)(2,1)S(1)}, bf16[48,1024]{1,0:T(8,128)(2,1)}, u32[]{:S(2)}) copy-start(bf16[48,1024]{1,0:T(8,128)(2,1)} %reduce-scatter.8.cloned.1.call-done) | copy-start | bytes 294916
  233.4 8.5 %collective-permute-start.2 = (bf16[48,1024]{1,0:T(8,128)(2,1)}, bf16[48,1024]{1,0:T(8,128)(2,1)S(1)}, u32[]{:S(2)}, u32[]{:S(2)}) collective-permute-start(bf16[48,1024]{1,0:T(8,128)(2,1)} %reduce-scatter.18.cloned.1.call-done), channel_id=1, source_target_pairs={{0,0},{1,1},{2,8},{3,9},{4,16},{5,17},{6,24},{7,25},{8,2},{9,3},{1... | collective-permute-start | bytes 294920 | tf_op jit(solution)/shard_map/ppermute | solution.py:46
  240.1 76.2 %copy-start.2 = (f32[2048]{0:T(1024)S(1)}, f32[2048]{0:T(1024)}, u32[]{:S(2)}) copy-start(f32[2048]{0:T(1024)} %param.10) | copy-start | bytes 24580
  240.1 77.1 %copy-start.3 = (s32[1,128]{1,0:T(1,128)S(1)}, s32[1,128]{1,0:T(1,128)}, u32[]{:S(2)}) copy-start(s32[1,128]{1,0:T(1,128)} %param.9) | copy-start | bytes 1540
  241.8 74.5 %reduce-scatter.20.cloned.1.call-start = ((), (), s32[]{:S(2)}) async-start(), calls=%async_computation.16 | async-start | bytes 294912 | tf_op jit(solution)/shard_map/reduce_scatter | solution.py:122
  278.8 1.5 collective-permute-start.1
Sparse Core Ops, SparseCore 0:
  44.4 21.0 reduce-scatter.7
  67.8 26.4 reduce-scatter.15
  101.7 20.5 reduce-scatter.9
  124.5 22.5 reduce-scatter.11
  198.5 34.8 reduce-scatter.17
  242.0 36.7 reduce-scatter.13
  282.7 33.5 reduce-scatter.19
where the time goes:
time: 327 us; the launch traced here: 326 us
  blocking collectives  131 us (40%)
  waiting for transfers between devices  108 us (33%)
  matrix products  45.5 us (14%)
  between operations  15 us (5%)
  starting transfers between devices  13.1 us (4%)
  local copies, waits for them, and re-layouts  8.58 us (3%)
  other arithmetic  4.91 us (2%)
    reduce_scatter x4, waiting for transfers between devices, grp_total(): lax.psum_scatter(partial_value.astype(bf16), 'grp', scatter_dimension=0,...  39.4 us
    reduce_scatter x1, waiting for transfers between devices, shards(): lax.psum_scatter(term, 'seq', scatter_dimension=0, tiled=True).astype(f32)  35.1 us
    all_gather x1, blocking collectives, spread(): every = lax.all_gather(swap(cols), 'seq', axis=0)  27.1 us
    dot_general x11, matrix products, matmul(): return jnp.dot(a, b, preferred_element_type=f32)  25.2 us
    reduce_scatter x2, waiting for transfers between devices, column_total(): lax.psum_scatter(part, 'seq', scatter_dimension=0, tiled=True)  24.2 us
    dot_general x4, matrix products, matmul_t(): lax.dot_general(a, b, (((1,), (1,)), ((), ())), preferred_element_type=f32)  20.3 us
    all_gather x1, blocking collectives, shards(): grad_gate = lax.all_gather(grad_gate, 'grp', axis=0, tiled=True)  18.2 us
    all_gather x1, blocking collectives, shards(): grad_up = lax.all_gather(grad_up, 'grp', axis=0, tiled=True)  17.4 us
  transfers between devices with their start and end apart: 12, of which 7 were waited for; matrix products, arithmetic and copies ran while one was open for 11% of the time, Pallas kernels for 0%

commit v1 on v0

--- a/solution.py
+++ b/solution.py
@@ -7,6 +7,23 @@
 norm_eps = 1e-06
 bf16 = jnp.bfloat16
 f32 = jnp.float32
+
+
+def joined_along(tiles, dim):
+    tiles = jnp.moveaxis(tiles, 0, dim)
+    shape = tiles.shape
+    return tiles.reshape(*shape[:dim], shape[dim] * shape[dim + 1], *shape[dim + 2 :])
+
+
+def gather_around(value, axis, dim):
+    length = lax.axis_size(axis)
+    right = [(i, (i + 1) % length) for i in range(length)]
+    blocks = [value]
+    while len(blocks) < length:
+        blocks.append(lax.ppermute(blocks[-1], axis, right))
+    index = lax.axis_index(axis)
+    blocks = jnp.stack(blocks)[(index - jnp.arange(length)) % length]
+    return joined_along(blocks, dim)
 
 
 def silu_parts(gate_value):
@@ -113,7 +130,7 @@
         grad_cols = lax.dynamic_slice_in_dim(out_grad[0], seq_at * width, width, 1)
         grad_cols = matmul(selector, grad_cols)
         grad_x = (back_cols + grad_cols).astype(bf16)
-        grad_x = lax.all_gather(grad_x, "grp", axis=0, tiled=True)
+        grad_x = gather_around(grad_x, "grp", 0)
         term = matmul_t(grad_x, w_in).astype(bf16)
         term = lax.all_to_all(
             term.reshape(grps, rows, feat), "grp", split_axis=0, concat_axis=1

time: 327 us -> 354 us (1.083)
  waiting for transfers between devices: 108 us -> 141 us
  blocking collectives: 131 us -> 122 us
    reduce_scatter x2, waiting for transfers between devices: 24.2 us -> 46.1 us  [column_total(): lax.psum_scatter(part, 'seq', scatter_dimension=0, tiled=True)]
    all_gather x1 -> x0, blocking collectives: 16.2 us -> none  [shards(): grad_x = lax.all_gather(grad_x, 'grp', axis=0, tiled=True)]
    ppermute x0 -> x3, waiting for transfers between devices: none -> 11.6 us  [gather_around(): blocks.append(lax.ppermute(blocks[-1], axis, right))]
    all_gather x1, blocking collectives: 16.8 us -> 26.6 us  [shards(): hidden = lax.all_gather(hidden, 'grp', axis=0, tiled=True)]
  transfers between devices with their start and end apart: 12 -> 15, of which waited for: 7 -> 9; matrix products, arithmetic and copies ran while one was open for 11% -> 10% of each run, Pallas kernels for 0% -> 0%
where the time goes in v1:
time: 354 us; the launch traced here: 353 us
  waiting for transfers between devices  141 us (40%)
  blocking collectives  122 us (34%)
  matrix products  45.5 us (13%)
  between operations  15 us (4%)
  starting transfers between devices  14.8 us (4%)
  local copies, waits for them, and re-layouts  9.15 us (3%)
  other arithmetic  4.98 us (1%)
    reduce_scatter x2, waiting for transfers between devices, column_total(): lax.psum_scatter(part, 'seq', scatter_dimension=0, tiled=True)  46.1 us
    reduce_scatter x4, waiting for transfers between devices, grp_total(): lax.psum_scatter(partial_value.astype(bf16), 'grp', scatter_dimension=0,...  39.4 us
    reduce_scatter x1, waiting for transfers between devices, shards(): lax.psum_scatter(term, 'seq', scatter_dimension=0, tiled=True).astype(f32)  35.1 us
    all_gather x1, blocking collectives, spread(): every = lax.all_gather(swap(cols), 'seq', axis=0)  27.1 us
    all_gather x1, blocking collectives, shards(): hidden = lax.all_gather(hidden, 'grp', axis=0, tiled=True)  26.6 us
    dot_general x11, matrix products, matmul(): return jnp.dot(a, b, preferred_element_type=f32)  25.2 us
    dot_general x4, matrix products, matmul_t(): lax.dot_general(a, b, (((1,), (1,)), ((), ())), preferred_element_type=f32)  20.3 us
    all_gather x1, blocking collectives, shards(): grad_gate = lax.all_gather(grad_gate, 'grp', axis=0, tiled=True)  18.2 us
  transfers between devices with their start and end apart: 15, of which 9 were waited for; matrix products, arithmetic and copies ran while one was open for 10% of the time, Pallas kernels for 0%

profile of v1, /device:TPU:0, one launch (start us, length us, event | category | flops | bytes accessed | tf_op | source)
XLA Modules:
  0.0 352.6 jit_solution(3769620022178258324)
XLA Ops:
  7.2 1.4 multiply_reduce_fusion.1
  8.6 1.3 reduce_max.9
  10.6 0.8 multiply_convert_fusion
  11.4 11.3 %all-gather.2 = bf16[8,9,2048]{2,1,0:T(8,128)(2,1)S(1)} all-gather(bf16[1,9,2048]{2,1,0:T(8,128)(2,1)S(1)} %pad_bitcast_fusion), channel_id=2, replica_groups=mesh['grp'=4,'seq'=8] {'seq'}, dimensions={0}, use_global_device_ids=true | all-gather | bytes 331776 | tf_op jit(solution)/shard_map/all_gather | solution.py:78
  23.8 0.7 copy.19
  24.5 4.9 %all-to-all-start = ((bf16[1,48,4,512]{3,1,0,2:T(8,128)(2,1)}), bf16[1,48,4,512]{3,1,0,2:T(8,128)(2,1)S(1)}, u32[]{:S(2)}, u32[]{:S(2)}) async-start(bf16[1,48,4,512]{3,1,0,2:T(8,128)(2,1)} %copy.19), calls=%async_computation | async-start | bytes 393216 | tf_op jit(solution)/shard_map/all_to_all | solution.py:90
  29.4 1.5 copy.29
  30.9 0.8 dynamic-slice_reduce_fusion
  31.9 0.7 copy.23
  32.6 4.8 %all-to-all-done = bf16[1,48,4,512]{3,1,0,2:T(8,128)(2,1)S(1)} async-done(((bf16[1,48,4,512]{3,1,0,2:T(8,128)(2,1)}), bf16[1,48,4,512]{3,1,0,2:T(8,128)(2,1)S(1)}, u32[]{:S(2)}, u32[]{:S(2)}) %all-to-all-start) | async-done | bytes 196640 | tf_op jit(solution)/shard_map/all_to_all | solution.py:90
  37.4 3.3 all-to-all-start.1
  40.7 1.1 convolution_convert_fusion.7
  41.9 4.5 %all-to-all-done.1 = bf16[1,48,4,256]{3,1,0,2:T(8,128)(2,1)S(1)} async-done(((bf16[1,48,4,256]{3,1,0,2:T(8,128)(2,1)}), bf16[1,48,4,256]{3,1,0,2:T(8,128)(2,1)S(1)}, u32[]{:S(2)}, u32[]{:S(2)}) %all-to-all-start.1) | async-done | bytes 98336 | tf_op jit(solution)/shard_map/all_to_all | solution.py:100
  46.5 11.9 %all_gather.29 = bf16[192,2048]{1,0:T(8,128)(2,1)S(1)} all-gather(bf16[192,256]{1,0:T(8,128)(2,1)S(1)} %bitcast.102), channel_id=1, replica_groups=mesh['grp'=4,'seq'=8] {'seq'}, dimensions={1}, use_global_device_ids=true | all-gather | bytes 884736 | tf_op jit(solution)/shard_map/all_gather | solution.py:103
  58.4 7.2 %convolution_convert_fusion = bf16[192,2048]{1,0:T(8,128)(2,1)} fusion(bf16[192,2048]{1,0:T(8,128)(2,1)S(1)} %all_gather.29, bf16[2048,2048]{1,0:T(8,128)(2,1)} %param.14), kind=kOutput, calls=%fused_computation.2 | convolution fusion | flops 1611005952 | bytes 9961472 | tf_op jit(solution)/shard_map/dot_general | solution.py:39
  65.7 1.6 collective-permute-start
  67.3 27.1 %all-gather.1 = bf16[384,1024]{1,0:T(8,128)(2,1)S(1)} all-gather(bf16[48,1024]{1,0:T(8,128)(2,1)S(1)} %collective-permute-done), channel_id=3, replica_groups=mesh['grp'=4,'seq'=8] {'seq'}, dimensions={0}, use_global_device_ids=true | all-gather | bytes 884736 | tf_op jit(solution)/shard_map/all_gather | solution.py:107
  94.4 0.8 copy.20
  95.5 6.1 %convolution_convert_fusion.3 = bf16[192,2048]{1,0:T(8,128)(2,1)} fusion(bf16[192,2048]{1,0:T(8,128)(2,1)S(1)} %bitcast.95, bf16[2048,2048]{1,0:T(8,128)(2,1)} %param.12), kind=kOutput, calls=%fused_computation.5 | convolution fusion | flops 1611005952 | bytes 9961472 | tf_op jit(solution)/shard_map/dot_general | solution.py:35
  101.6 6.1 %convolution_convert_fusion.2 = bf16[192,2048]{1,0:T(8,128)(2,1)} fusion(bf16[192,2048]{1,0:T(8,128)(2,1)S(1)} %bitcast.96, bf16[2048,2048]{1,0:T(8,128)(2,1)} %param.13), kind=kOutput, calls=%fused_computation.4 | convolution fusion | flops 1611005952 | bytes 9961472 | tf_op jit(solution)/shard_map/dot_general | solution.py:35
  107.8 14.5 %reduce-scatter.10.cloned.1.call-done = bf16[48,2048]{1,0:T(8,128)(2,1)} async-done(((bf16[192,2048]{1,0:T(8,128)(2,1)}), bf16[48,2048]{1,0:T(8,128)(2,1)}) %reduce-scatter.10.cloned.1.call-update) | async-done | bytes 196624 | tf_op jit(solution)/shard_map/reduce_scatter | solution.py:53
  122.3 24.9 %reduce-scatter.12.cloned.1.call-done = bf16[48,2048]{1,0:T(8,128)(2,1)} async-done(((bf16[192,2048]{1,0:T(8,128)(2,1)}), bf16[48,2048]{1,0:T(8,128)(2,1)}) %reduce-scatter.12.cloned.1.call-update) | async-done | bytes 196624 | tf_op jit(solution)/shard_map/reduce_scatter | solution.py:53
  147.1 1.4 fusion.8
  148.5 18.2 %all_gather.30 = bf16[192,2048]{1,0:T(8,128)(2,1)S(1)} all-gather(bf16[48,2048]{1,0:T(8,128)(2,1)S(1)} %get-tuple-element.3), channel_id=1, replica_groups=mesh['grp'=4,'seq'=8] {'grp'}, dimensions={0}, use_global_device_ids=true | all-gather | bytes 983040 | tf_op jit(solution)/shard_map/all_gather | solution.py:123
  166.7 6.3 %fusion.45 = f32[192,2048]{1,0:T(8,128)S(1)} fusion(bf16[192,2048]{1,0:T(8,128)(2,1)S(1)} %all_gather.30, bf16[2048,2048]{1,0:T(8,128)(2,1)} %param.12), kind=kOutput, calls=%fused_computation.82 | convolution fusion | flops 1610612736 | bytes 10747904 | tf_op jit(solution)/shard_map/dot_general | solution.py:39
  173.0 17.4 %all_gather.31 = bf16[192,2048]{1,0:T(8,128)(2,1)S(1)} all-gather(bf16[48,2048]{1,0:T(8,128)(2,1)S(1)} %get-tuple-element.2), channel_id=1, replica_groups=mesh['grp'=4,'seq'=8] {'grp'}, dimensions={0}, use_global_device_ids=true | all-gather | bytes 983040 | tf_op jit(solution)/shard_map/all_gather | solution.py:124
  190.4 6.3 %fusion = bf16[192,2048]{1,0:T(8,128)(2,1)S(1)} fusion(f32[192,2048]{1,0:T(8,128)S(1)} %fusion.45, bf16[192,2048]{1,0:T(8,128)(2,1)S(1)} %all_gather.31, bf16[2048,2048]{1,0:T(8,128)(2,1)} %param.13), kind=kOutput, calls=%fused_computation.6 | convolution fusion | flops 1611399168 | bytes 11534336 | tf_op jit(solution)/shard_map/dot_general | solution.py:39
  196.7 0.6 reshape.167
  197.2 1.1 copy.24
  198.4 35.0 %reduce-scatter.18.cloned.1.call-done = bf16[48,1024]{1,0:T(8,128)(2,1)} async-done(((bf16[384,1024]{1,0:T(8,128)(2,1)}), bf16[48,1024]{1,0:T(8,128)(2,1)}) %reduce-scatter.18.cloned.1.call-update) | async-done | bytes 98320 | tf_op jit(solution)/shard_map/reduce_scatter | solution.py:114
  233.4 1.5 collective-permute-start.2
  234.9 26.6 %all_gather.28 = bf16[192,2048]{1,0:T(8,128)(2,1)S(1)} all-gather(bf16[48,2048]{1,0:T(8,128)(2,1)S(1)} %get-tuple-element.4), channel_id=1, replica_groups=mesh['grp'=4,'seq'=8] {'grp'}, dimensions={0}, use_global_device_ids=true | all-gather | bytes 983040 | tf_op jit(solution)/shard_map/all_gather | solution.py:125
  261.5 1.1 add_convert_fusion
  262.6 5.2 %convolution_convert_fusion.1 = bf16[192,2048]{1,0:T(8,128)(2,1)S(1)} fusion(bf16[192,2048]{1,0:T(8,128)(2,1)S(1)} %all_gather.28, bf16[2048,2048]{1,0:T(8,128)(2,1)} %param.14), kind=kOutput, calls=%fused_computation.3 | convolution fusion | flops 1611005952 | bytes 9961472 | tf_op jit(solution)/shard_map/dot_general | solution.py:35
  267.8 0.6 reshape.164
  268.4 1.1 copy.21
  269.6 1.7 collective-permute-start.4
  271.3 5.1 %collective-permute-done.4 = bf16[48,1024]{1,0:T(8,128)(2,1)S(1)} collective-permute-done((bf16[48,1024]{1,0:T(8,128)(2,1)S(1)}, bf16[48,1024]{1,0:T(8,128)(2,1)S(1)}, u32[]{:S(2)}, u32[]{:S(2)}) %collective-permute-start.4) | collective-permute-done | bytes 98336 | tf_op jit(solution)/shard_map/ppermute | solution.py:23
  276.4 6.5 %collective-permute-done.5 = bf16[48,1024]{1,0:T(8,128)(2,1)S(1)} collective-permute-done((bf16[48,1024]{1,0:T(8,128)(2,1)S(1)}, bf16[48,1024]{1,0:T(8,128)(2,1)S(1)}, u32[]{:S(2)}, u32[]{:S(2)}) %collective-permute-start.5) | collective-permute-done | bytes 98336 | tf_op jit(solution)/shard_map/ppermute | solution.py:23
  282.9 0.6 gather_fusion
  284.0 9.2 %all_to_all.45 = bf16[4,48,1,512]{3,1,2,0:T(8,128)(2,1)S(1)} all-to-all(bf16[4,48,1,512]{3,1,2,0:T(8,128)(2,1)S(1)} %bitcast.93), channel_id=1, replica_groups=mesh['grp'=4,'seq'=8] {'grp'}, dimensions={0} | all-to-all | bytes 393216 | tf_op jit(solution)/shard_map/all_to_all | solution.py:135
  293.4 1.0 convolution_convert_fusion.5
  294.4 11.1 %reduce-scatter.14.cloned.1.call-done = bf16[48,1024]{1,0:T(8,128)(2,1)} async-done(((bf16[384,1024]{1,0:T(8,128)(2,1)}), bf16[48,1024]{1,0:T(8,128)(2,1)}) %reduce-scatter.14.cloned.1.call-update) | async-done | bytes 98320 | tf_op jit(solution)/shard_map/reduce_scatter | solution.py:114
  305.5 1.5 collective-permute-start.1
  307.0 0.9 fusion.2
  307.9 35.1 %reduce-scatter.20.cloned.1.call-done = bf16[8,2048]{1,0:T(8,128)(2,1)} async-done(((bf16[64,2048]{1,0:T(8,128)(2,1)}), bf16[8,2048]{1,0:T(8,128)(2,1)}) %reduce-scatter.20.cloned.1.call-update) | async-done | bytes 32784 | tf_op jit(solution)/shard_map/reduce_scatter | solution.py:139
  343.0 0.9 multiply_reduce_fusion
  343.9 1.9 fusion.1
  (52 shorter events, 2.8 us)
Async XLA Ops:
  7.2 33.6 %copy-start = (bf16[512,1024]{1,0:T(8,128)(2,1)S(1)}, bf16[512,1024]{1,0:T(8,128)(2,1)}, u32[]{:S(2)}) copy-start(bf16[512,1024]{1,0:T(8,128)(2,1)} %param.11) | copy-start | bytes 3145732
  24.5 12.9 %all-to-all-start = ((bf16[1,48,4,512]{3,1,0,2:T(8,128)(2,1)}), bf16[1,48,4,512]{3,1,0,2:T(8,128)(2,1)S(1)}, u32[]{:S(2)}, u32[]{:S(2)}) async-start(bf16[1,48,4,512]{3,1,0,2:T(8,128)(2,1)} %copy.19), calls=%async_computation | async-start | bytes 393216 | tf_op jit(solution)/shard_map/all_to_all | solution.py:90
  37.4 9.1 %all-to-all-start.1 = ((bf16[1,48,4,256]{3,1,0,2:T(8,128)(2,1)}), bf16[1,48,4,256]{3,1,0,2:T(8,128)(2,1)S(1)}, u32[]{:S(2)}, u32[]{:S(2)}) async-start(bf16[1,48,4,256]{3,1,0,2:T(8,128)(2,1)} %copy.23), calls=%async_computation.5 | async-start | bytes 196608 | tf_op jit(solution)/shard_map/all_to_all | solution.py:100
  40.7 25.1 %reduce-scatter.8.cloned.1.call-start = ((), (), s32[]{:S(2)}) async-start(), calls=%async_computation.10 | async-start | bytes 491520 | tf_op jit(solution)/shard_map/reduce_scatter | solution.py:53
  41.9 65.9 %reduce-scatter.16.cloned.1.call-start = ((), (), s32[]{:S(2)}) async-start(), calls=%async_computation.14 | async-start | bytes 983040 | tf_op jit(solution)/shard_map/reduce_scatter | solution.py:53
  65.7 56.6 %reduce-scatter.10.cloned.1.call-start = ((), (), s32[]{:S(2)}) async-start(), calls=%async_computation.11 | async-start | bytes 983040 | tf_op jit(solution)/shard_map/reduce_scatter | solution.py:53
  65.7 1.6 collective-permute-start
  101.6 45.6 %reduce-scatter.12.cloned.1.call-start = ((), (), s32[]{:S(2)}) async-start(), calls=%async_computation.12 | async-start | bytes 983040 | tf_op jit(solution)/shard_map/reduce_scatter | solution.py:53
  107.7 125.6 %reduce-scatter.18.cloned.1.call-start = ((), (), s32[]{:S(2)}) async-start(), calls=%async_computation.15 | async-start | bytes 884736 | tf_op jit(solution)/shard_map/reduce_scatter | solution.py:114
  198.4 107.1 %reduce-scatter.14.cloned.1.call-start = ((), (), s32[]{:S(2)}) async-start(), calls=%async_computation.13 | async-start | bytes 884736 | tf_op jit(solution)/shard_map/reduce_scatter | solution.py:114
  233.4 28.1 %collective-permute-start.2 = (bf16[48,1024]{1,0:T(8,128)(2,1)}, bf16[48,1024]{1,0:T(8,128)(2,1)S(1)}, u32[]{:S(2)}, u32[]{:S(2)}) collective-permute-start(bf16[48,1024]{1,0:T(8,128)(2,1)} %reduce-scatter.18.cloned.1.call-done), channel_id=1, source_target_pairs={{0,0},{1,1},{2,8},{3,9},{4,16},{5,17},{6,24},{7,25},{8,2},{9,3},{1... | collective-permute-start | bytes 294920 | tf_op jit(solution)/shard_map/ppermute | solution.py:63
  262.5 7.1 %collective-permute-start.3 = (bf16[48,1024]{1,0:T(8,128)(2,1)S(1)}, bf16[48,1024]{1,0:T(8,128)(2,1)S(1)}, u32[]{:S(2)}, u32[]{:S(2)}) collective-permute-start(bf16[48,1024]{1,0:T(8,128)(2,1)S(1)} %add_convert_fusion), channel_id=1, source_target_pairs={{0,8},{8,16},{16,24},{24,0},{1,9},{9,17},{17,25},{25,1},{2,10},{10... | collective-permute-start | bytes 294920 | tf_op jit(solution)/shard_map/ppermute | solution.py:23
  267.8 39.2 %copy-start.1 = (bf16[48,1024]{1,0:T(8,128)(2,1)S(1)}, bf16[48,1024]{1,0:T(8,128)(2,1)}, u32[]{:S(2)}) copy-start(bf16[48,1024]{1,0:T(8,128)(2,1)} %reduce-scatter.8.cloned.1.call-done) | copy-start | bytes 294916
  267.8 75.2 %copy-start.2 = (f32[2048]{0:T(1024)S(1)}, f32[2048]{0:T(1024)}, u32[]{:S(2)}) copy-start(f32[2048]{0:T(1024)} %param.10) | copy-start | bytes 24580
  267.8 76.0 %copy-start.3 = (s32[1,128]{1,0:T(1,128)S(1)}, s32[1,128]{1,0:T(1,128)}, u32[]{:S(2)}) copy-start(s32[1,128]{1,0:T(1,128)} %param.9) | copy-start | bytes 1540
  269.5 73.4 %reduce-scatter.20.cloned.1.call-start = ((), (), s32[]{:S(2)}) async-start(), calls=%async_computation.16 | async-start | bytes 294912 | tf_op jit(solution)/shard_map/reduce_scatter | solution.py:139
  269.6 6.8 %collective-permute-start.4 = (bf16[48,1024]{1,0:T(8,128)(2,1)S(1)}, bf16[48,1024]{1,0:T(8,128)(2,1)S(1)}, u32[]{:S(2)}, u32[]{:S(2)}) collective-permute-start(bf16[48,1024]{1,0:T(8,128)(2,1)S(1)} %collective-permute-done.3), channel_id=1, source_target_pairs={{0,8},{8,16},{16,24},{24,0},{1,9},{9,17},{17,25},{25,1},{2,10},{10... | collective-permute-start | bytes 294920 | tf_op jit(solution)/shard_map/ppermute | solution.py:23
  276.4 6.5 %collective-permute-start.5 = (bf16[48,1024]{1,0:T(8,128)(2,1)S(1)}, bf16[48,1024]{1,0:T(8,128)(2,1)S(1)}, u32[]{:S(2)}, u32[]{:S(2)}) collective-permute-start(bf16[48,1024]{1,0:T(8,128)(2,1)S(1)} %collective-permute-done.4), channel_id=1, source_target_pairs={{0,8},{8,16},{16,24},{24,0},{1,9},{9,17},{17,25},{25,1},{2,10},{10... | collective-permute-start | bytes 294920 | tf_op jit(solution)/shard_map/ppermute | solution.py:23
  305.5 1.5 collective-permute-start.1
Sparse Core Ops, SparseCore 0:
  44.4 21.0 reduce-scatter.7
  67.8 26.4 reduce-scatter.15
  101.7 20.5 reduce-scatter.9
  124.5 22.5 reduce-scatter.11
  198.5 34.8 reduce-scatter.17
  269.6 35.7 reduce-scatter.13
  309.4 33.5 reduce-scatter.19
